TPU v7x, 32 devices: a whole 2x2x4 slice. The times are simulated.
32 devices in a mesh: groups: 2 (over y), rows: 4 (over x, core), cols: 4 (over z).
Axes of the slice: x: 2, y: 2, z: 4, core: 2. Of those that a mesh axis runs over, the one named last changes fastest.
Arguments:
- pair_rep: float32 [384, 192, 128], P(('groups', 'cols'), 'rows'), parts along dimension 0, may hold values from -6 to 6
- token_mask: int32 [384], P(('groups', 'rows')), parts along dimension 0, may hold values from 0 to 1, as said below
- norm_gain: float32 [128], replicated, may hold values from 0.1 to 1.9
- norm_shift: float32 [128], replicated, may hold values from -3 to 3
- w_query: bfloat16 [128, 128], replicated, may hold values from -0.5 to 0.5
- w_keyval: bfloat16 [128, 256], replicated, may hold values from -0.5 to 0.5
- w_gate: bfloat16 [128, 128], replicated, may hold values from -0.5 to 0.5
- gate_shift: float32 [128], replicated, may hold values from -3 to 3
- w_bias: float32 [128, 4], replicated, may hold values from -12 to 12
- w_out: bfloat16 [128, 128], replicated, may hold values from -0.5 to 0.5
- out_shift: float32 [128], replicated, may hold values from -3 to 3
Outputs:
- pair_update: float32 [384, 192, 128], P(('groups', 'cols'), 'rows'), parts along dimension 0
There are 2 independent parts, one for each index of `groups`. A program takes and returns all parts, laid end to end along the dimension named above; an argument that names none is the same for every part. Nothing has to cross between parts.
Inputs may be any that keep to these rules, and one draw needn't show every extreme that they name: `token_mask`: position 0 is always a valid residue and the last position never is.
All inputs are finite; a program needn't handle non-finite values.
Results may differ from a plain program's by a relative error of at most 0.012.
The roundings to bfloat16 on the way count: a program that leaves them out, or rounds other values in their place, can miss the bound.
Values may be sent and summed in bfloat16 or wider, within the bound.
No kernel may reach another device: no remote copies, remote signals or barrier semaphores. Data moves between devices by JAX's collectives and lax.ppermute only.
A program may use at most 128 MiB of HBM per device.

v0:
```python
import jax
import jax.numpy as jnp
from jax import lax
from jax.sharding import PartitionSpec as P

HEADS = 4
HEAD_DIM = 32


def layer_norm(values, norm_gain, norm_shift):
    mean_val = jnp.mean(values, axis=-1, keepdims=True)
    centred = values - mean_val
    variance = jnp.mean(centred * centred, axis=-1, keepdims=True)
    return (centred * lax.rsqrt(variance + 1e-05) * norm_gain + norm_shift).astype(jnp.bfloat16)


def largest_divisor(count, limit):
    return max(
        (candidate for candidate in range(1, min(count, limit) + 1) if count % candidate == 0)
    )


def whole_row_layer(
    normed, token_mask, w_query, w_keyval, w_gate, gate_shift, w_bias, w_out, out_shift
):
    width = normed.shape[2]
    local_bias = jnp.dot(
        normed.astype(jnp.float32), w_bias, precision=lax.Precision.HIGHEST
    ).transpose(2, 0, 1)
    wide = lax.all_to_all(normed, "rows", split_axis=0, concat_axis=1, tiled=True)
    few_rows, token_count, _ = wide.shape
    bias_part = lax.all_gather(local_bias, "cols", axis=1, tiled=True)
    full_bias, full_mask = (
        lax.all_gather(bias_part, "rows", axis=2, tiled=True),
        lax.all_gather(token_mask.astype(jnp.float32), "rows", axis=0, tiled=True),
    )
    queries = (
        jnp.dot(wide, w_query, preferred_element_type=jnp.float32) * HEAD_DIM ** (-0.5)
    ).astype(jnp.bfloat16)
    queries = queries.reshape(few_rows, token_count, HEADS, HEAD_DIM)
    keyvals = jnp.dot(wide, w_keyval, preferred_element_type=jnp.float32).astype(jnp.bfloat16)
    keys = keyvals[..., :width].reshape(few_rows, token_count, HEADS, HEAD_DIM)
    values = keyvals[..., width:].reshape(few_rows, token_count, HEADS, HEAD_DIM)
    gates = jax.nn.sigmoid(jnp.dot(wide, w_gate, preferred_element_type=jnp.float32) + gate_shift)
    usable = full_mask > 0.5
    block_len = largest_divisor(token_count, 128)

    def one_block(block_index, gated_all):
        start = block_index * block_len
        query_block = lax.dynamic_slice_in_dim(queries, start, block_len, 1)
        bias_block = lax.dynamic_slice_in_dim(full_bias, start, block_len, 1)
        gate_block = lax.dynamic_slice_in_dim(gates, start, block_len, 1)
        scores = jnp.einsum(
            "ijhd,ikhd->hijk", query_block, keys, preferred_element_type=jnp.float32
        )
        scores = scores + bias_block[:, None]
        scores = jnp.where(usable[None, None, None, :], scores, jnp.float32(-1000000000.0))
        highest = jnp.max(scores, axis=-1, keepdims=True)
        expo = jnp.exp(scores - highest)
        total = jnp.sum(expo, axis=-1)
        weights = expo.astype(jnp.bfloat16)
        mixed = jnp.einsum("hijk,ikhd->ijhd", weights, values, preferred_element_type=jnp.float32)
        attended = mixed / total.transpose(1, 2, 0)[..., None]
        gated = (gate_block * attended.reshape(few_rows, block_len, width)).astype(jnp.bfloat16)
        return lax.dynamic_update_slice_in_dim(gated_all, gated, start, 1)

    gated_all = lax.fori_loop(
        0,
        token_count // block_len,
        one_block,
        jnp.zeros((few_rows, token_count, width), jnp.bfloat16),
    )
    gated_home = lax.all_to_all(gated_all, "rows", split_axis=1, concat_axis=0, tiled=True)
    return jnp.dot(gated_home, w_out, preferred_element_type=jnp.float32) + out_shift


def on_device(
    pair_rep,
    token_mask,
    norm_gain,
    norm_shift,
    w_query,
    w_keyval,
    w_gate,
    gate_shift,
    w_bias,
    w_out,
    out_shift,
):
    normed = layer_norm(pair_rep, norm_gain, norm_shift)
    return whole_row_layer(
        normed, token_mask, w_query, w_keyval, w_gate, gate_shift, w_bias, w_out, out_shift
    )


def solution(mesh):
    return jax.shard_map(
        on_device,
        mesh=mesh,
        in_specs=(
            P(("groups", "cols"), "rows", None),
            P(("groups", "rows")),
            P(),
            P(),
            P(),
            P(),
            P(),
            P(),
            P(),
            P(),
            P(),
        ),
        out_specs=P(("groups", "cols"), "rows", None),
        check_vma=False,
    )
```

profile of v0, /device:TPU:0, one launch (start us, length us, event | category | flops | bytes accessed | tf_op | source)
XLA Modules:
  0.0 85.9 jit_solution(3610924705760710887)
XLA Ops:
  0.0 0.0 copy-start
  0.0 1.7 %reduce_sum.31 = f32[48,48]{1,0:T(8,128)S(1)} reduce(f32[48,48,128]{2,1,0:T(8,128)} %param.13, f32[]{:T(128)} %constant.58.clone.1), dimensions={2}, to_apply=%region_0.0 | reduce | flops 292608 | bytes 1188868 | tf_op jit(solution)/shard_map/reduce_sum | solution.py:11
  1.8 0.0 copy-done.1
  1.8 0.7 multiply_reduce_fusion
  2.5 0.0 copy-done.9
  2.5 0.0 copy-done.8
  2.5 0.0 copy-start.7
  2.5 1.5 %add_convert_fusion = bf16[48,48,128]{2,1,0:T(8,128)(2,1)} fusion(f32[48,48,128]{2,1,0:T(8,128)S(1)} %copy-done.1, f32[128]{0:T(128)S(1)} %copy-done.8, f32[128]{0:T(128)S(1)} %copy-done.9, f32[48,48]{1,0:T(8,128)S(1)} %add_rsqrt_fusion, f32[48,48]{1,0:T(8,128)S(1)} %broadcast_multiply_fusion), kind=kLoop, calls=%fused_computation.31 | loop fusion | flops 1474560 | bytes 1788928 | tf_op jit(solution)/shard_map/convert_element_type | solution.py:14
  4.0 4.2 %all-to-all-start = ((bf16[48,48,128]{2,1,0:T(8,128)(2,1)}), bf16[48,48,128]{2,1,0:T(8,128)(2,1)S(1)}, u32[]{:S(2)}, u32[]{:S(2)}) async-start(bf16[48,48,128]{2,1,0:T(8,128)(2,1)} %add_convert_fusion), calls=%async_computation | async-start | bytes 1179648 | tf_op jit(solution)/shard_map/all_to_all | solution.py:30
  8.3 0.0 copy-done.7
  8.3 2.8 %convolution_bitcast_fusion = f32[4,48,48]{2,0,1:T(4,128)S(1)} fusion(bf16[48,48,128]{2,1,0:T(8,128)(2,1)} %add_convert_fusion, f32[128,4]{0,1:T(4,128)S(1)} %copy-done.7), kind=kOutput, calls=%fused_computation.33 | convolution fusion | flops 14155776 | bytes 628736 | tf_op jit(solution)/shard_map/dot_general | solution.py:27
  11.1 15.8 %all_gather.10 = f32[4,192,48]{2,0,1:T(4,128)S(1)} all-gather(f32[4,48,48]{2,0,1:T(4,128)S(1)} %convolution_bitcast_fusion), channel_id=1, replica_groups=mesh['groups'=2,'rows'=4,'cols'=4] {'cols'}, dimensions={1}, use_global_device_ids=true | all-gather | bytes 184320 | tf_op jit(solution)/shard_map/all_gather | solution.py:32
  27.0 0.2 copy.36
  27.2 0.0 copy-done.14
  27.2 0.6 dynamic-slice
  28.3 0.0 copy-done.12
  28.3 0.1 convert_dynamic-update-slice_fusion
  28.4 5.6 %all-reduce = f32[192]{0:T(256)S(1)} all-reduce(f32[192]{0:T(256)S(1)} %convert_dynamic-update-slice_fusion), channel_id=1, replica_groups=mesh['groups'=2,'rows'=4,'cols'=4] {'rows'}, use_global_device_ids=true, to_apply=%add | all-reduce | flops 192 | bytes 1536
  34.1 9.0 %all_gather.11 = f32[4,192,192]{1,0,2:T(4,128)S(1)} all-gather(f32[4,192,48]{1,0,2:T(4,128)S(1)} %copy.36), channel_id=1, replica_groups=mesh['groups'=2,'rows'=4,'cols'=4] {'rows'}, dimensions={2}, use_global_device_ids=true | all-gather | bytes 737280 | tf_op jit(solution)/shard_map/all_gather | solution.py:34
  43.1 0.0 all-to-all-done
  43.1 0.1 copy.33
  43.2 0.0 copy-done
  43.2 0.4 convolution_convert_fusion
  43.7 0.3 fusion.39
  44.0 0.3 copy.35
  44.3 0.0 copy-start.6
  44.3 0.9 %copy.40 = bf16[12,192,4,32]{1,3,0,2:T(8,128)(2,1)} copy(bf16[12,192,4,32]{1,3,2,0:T(8,128)(2,1)S(1)} %bitcast.59) | data formatting | bytes 1179648 | tf_op jit(solution)/shard_map/while | solution.py:67
  45.2 1.2 %copy.37 = bf16[12,192,128]{1,2,0:T(8,128)(2,1)} copy(bf16[12,192,128]{2,1,0:T(8,128)(2,1)S(1)} %get-tuple-element.188) | data formatting | bytes 1179648 | tf_op jit(solution)/shard_map/slice | solution.py:43
  46.4 0.0 copy-done.6
  46.4 0.3 fusion.28
  46.7 1.2 %copy.34 = bf16[12,192,128]{1,2,0:T(8,128)(2,1)} copy(bf16[12,192,128]{2,1,0:T(8,128)(2,1)S(1)} %fusion.28) | data formatting | bytes 1179648 | tf_op jit(solution)/shard_map/convert_element_type | solution.py:39
  47.9 0.0 copy-done.11
  47.9 0.0 copy-done.13
  47.9 1.5 %fusion.27 = f32[12,192,128]{2,1,0:T(8,128)} fusion(bf16[12,192,128]{2,1,0:T(8,128)(2,1)S(1)} %bitcast.58, f32[128]{0:T(128)S(1)} %copy-done.13, bf16[128,128]{1,0:T(8,128)(2,1)S(1)} %copy-done.11), kind=kOutput, calls=%fused_computation.29 | convolution fusion | flops 76677120 | bytes 1802752 | tf_op jit(solution)/shard_map/dot_general | solution.py:44
  49.3 1.0 %broadcast_in_dim.45.clone = bf16[12,192,128]{2,0,1:T(8,128)(2,1)} broadcast(bf16[]{:T(256)} %constant.57.clone.1), dimensions={} | broadcast | bytes 589826 | tf_op jit(solution)/shard_map/broadcast_in_dim | solution.py:71
  50.3 0.0 copy-done.3
  50.3 18.9 %while.13 = (s32[]{:T(128)}, bf16[12,192,128]{2,0,1:T(8,128)(2,1)}, f32[12,192,128]{2,1,0:T(8,128)}, pred[192]{0:T(512)(128)(4,1)S(1)}, bf16[12,192,4,32]{1,3,2,...) while((s32[]{:T(128)}, bf16[12,192,128]{2,0,1:T(8,128)(2,1)}, ...), condition=%wide.region_5.6_spmd, body=%wide.region_2.5_spmd.sunk | while | flops 118112448 | bytes 19440052 | solution.py:67
  50.3 0.3 constant_dynamic-slice_fusion.13
  50.6 0.2 copy.78
  50.8 4.4 %fusion.59 = (f32[4,12,96]{2,1,0:T(8,128)S(1)}, bf16[4,12,96,192]{3,2,1,0:T(8,128)(2,1)}) fusion(f32[4,96,192]{2,1,0:T(8,128)S(1)} %copy.78, pred[192]{0:T(512)(128)(4,1)S(1)} %get-tuple-element.270, bf16[12,192,4,32]{1,3,0,2:T(8,128)(2,1)S(1)} %get-tuple-element.272, bf16[12,192,4,32]{1,3,2,0:T(8,128)(2,1)} %get-tuple-element.271, s32[]{:T(128)S(6)} %select_n.31), kind=kOutput, calls=%fused_computation.43.clone.1 | convolution fusion | flops 61046976 | bytes 3066052 | tf_op jit(solution)/shard_map/while/body/eval_jaxpr/sub | solution.py:59
  55.3 0.0 copy-start.2
  55.3 2.9 %fusion.60 = f32[12,96,4,32]{1,3,2,0:T(8,128)S(1)} fusion(bf16[12,192,4,32]{1,3,2,0:T(8,128)(2,1)} %get-tuple-element.274, bf16[4,12,96,192]{3,2,1,0:T(8,128)(2,1)} %get-tuple-element.241, f32[12,96,4]{1,2,0:T(4,128)S(1)} %copy.79), kind=kOutput, calls=%fused_computation.10.clone.1 | convolution fusion | flops 56770560 | bytes 2967552 | tf_op jit(solution)/shard_map/while/body/eval_jaxpr/hijk,ikhd->ijhd/dot_general | solution.py:62
  58.2 0.0 copy-done.2
  58.2 0.1 constant_dynamic-slice_fusion.12
  58.3 0.3 copy.77
  58.5 0.1 fusion.61
  58.6 0.0 copy-start.4
  58.6 0.3 copy.80
  59.0 0.8 constant_dynamic-update-slice_fusion.2
  59.8 0.0 copy-done.4
  59.8 0.3 constant_dynamic-slice_fusion.13
  60.1 0.2 copy.78
  60.3 4.4 %fusion.59 = (f32[4,12,96]{2,1,0:T(8,128)S(1)}, bf16[4,12,96,192]{3,2,1,0:T(8,128)(2,1)}) fusion(f32[4,96,192]{2,1,0:T(8,128)S(1)} %copy.78, pred[192]{0:T(512)(128)(4,1)S(1)} %get-tuple-element.270, bf16[12,192,4,32]{1,3,0,2:T(8,128)(2,1)S(1)} %get-tuple-element.272, bf16[12,192,4,32]{1,3,2,0:T(8,128)(2,1)} %get-tuple-element.271, s32[]{:T(128)S(6)} %select_n.31), kind=kOutput, calls=%fused_computation.43.clone.1 | convolution fusion | flops 61046976 | bytes 3066052 | tf_op jit(solution)/shard_map/while/body/eval_jaxpr/sub | solution.py:59
  64.7 0.0 copy-start.2
  64.7 2.9 %fusion.60 = f32[12,96,4,32]{1,3,2,0:T(8,128)S(1)} fusion(bf16[12,192,4,32]{1,3,2,0:T(8,128)(2,1)} %get-tuple-element.274, bf16[4,12,96,192]{3,2,1,0:T(8,128)(2,1)} %get-tuple-element.241, f32[12,96,4]{1,2,0:T(4,128)S(1)} %copy.79), kind=kOutput, calls=%fused_computation.10.clone.1 | convolution fusion | flops 56770560 | bytes 2967552 | tf_op jit(solution)/shard_map/while/body/eval_jaxpr/hijk,ikhd->ijhd/dot_general | solution.py:62
  67.6 0.1 constant_dynamic-slice_fusion.12
  67.7 0.3 copy.77
  68.0 0.1 fusion.61
  68.1 0.3 copy.80
  68.4 0.8 constant_dynamic-update-slice_fusion.2
  69.2 0.0 copy-done.4
  69.2 15.2 %all_to_all.36 = bf16[12,192,128]{2,0,1:T(8,128)(2,1)S(1)} all-to-all(bf16[12,192,128]{2,0,1:T(8,128)(2,1)} %get-tuple-element.281), channel_id=1, replica_groups=mesh['groups'=2,'rows'=4,'cols'=4] {'rows'}, dimensions={1} | all-to-all | bytes 1179648 | tf_op jit(solution)/shard_map/all_to_all | solution.py:73
  84.4 0.2 copy.44
  84.6 1.3 %convolution_add_fusion = f32[48,48,128]{2,1,0:T(8,128)} fusion(bf16[48,48,128]{2,1,0:T(8,128)(2,1)S(1)} %bitcast.62, f32[128]{0:T(128)S(1)} %copy-done.10, bf16[128,128]{1,0:T(8,128)(2,1)S(1)} %copy-done.5), kind=kOutput, calls=%fused_computation.23 | convolution fusion | flops 75792384 | bytes 1802752 | tf_op jit(solution)/shard_map/dot_general | solution.py:74
  (20 shorter events, 0.1 us)
Async XLA Ops:
  0.0 43.2 %copy-start = (bf16[128,256]{1,0:T(8,128)(2,1)S(1)}, bf16[128,256]{1,0:T(8,128)(2,1)}, u32[]{:S(2)}) copy-start(bf16[128,256]{1,0:T(8,128)(2,1)} %param.18) | copy-start | bytes 196612
  0.0 1.8 %copy-start.1 = (f32[48,48,128]{2,1,0:T(8,128)S(1)}, f32[48,48,128]{2,1,0:T(8,128)}, u32[]{:S(2)}) copy-start(f32[48,48,128]{2,1,0:T(8,128)} %param.13) | copy-start | bytes 3538948
  0.0 2.5 %copy-start.9 = (f32[128]{0:T(128)S(1)}, f32[128]{0:T(128)}, u32[]{:S(2)}) copy-start(f32[128]{0:T(128)} %param.15) | copy-start | bytes 1540
  0.0 2.5 %copy-start.8 = (f32[128]{0:T(128)S(1)}, f32[128]{0:T(128)}, u32[]{:S(2)}) copy-start(f32[128]{0:T(128)} %param.16) | copy-start | bytes 1540
  2.5 5.8 %copy-start.7 = (f32[128,4]{0,1:T(4,128)S(1)}, f32[128,4]{0,1:T(4,128)}, u32[]{:S(2)}) copy-start(f32[128,4]{0,1:T(4,128)} %param.21) | copy-start | bytes 6148
  4.0 39.1 %all-to-all-start = ((bf16[48,48,128]{2,1,0:T(8,128)(2,1)}), bf16[48,48,128]{2,1,0:T(8,128)(2,1)S(1)}, u32[]{:S(2)}, u32[]{:S(2)}) async-start(bf16[48,48,128]{2,1,0:T(8,128)(2,1)} %add_convert_fusion), calls=%async_computation | async-start | bytes 1179648 | tf_op jit(solution)/shard_map/all_to_all | solution.py:30
  8.3 18.9 %copy-start.14 = (u32[32]{0:T(128)S(1)}, u32[32]{0:T(128)}, u32[]{:S(2)}) copy-start(u32[32]{0:T(128)} %constant.66) | copy-start | bytes 388
  8.3 20.1 %copy-start.12 = (s32[48]{0:T(128)S(1)}, s32[48]{0:T(128)}, u32[]{:S(2)}) copy-start(s32[48]{0:T(128)} %param.14) | copy-start | bytes 580
  44.3 2.1 %copy-start.6 = (bf16[128,128]{1,0:T(8,128)(2,1)S(1)}, bf16[128,128]{1,0:T(8,128)(2,1)}, u32[]{:S(2)}) copy-start(bf16[128,128]{1,0:T(8,128)(2,1)} %param.17) | copy-start | bytes 98308
  46.4 1.5 %copy-start.11 = (bf16[128,128]{1,0:T(8,128)(2,1)S(1)}, bf16[128,128]{1,0:T(8,128)(2,1)}, u32[]{:S(2)}) copy-start(bf16[128,128]{1,0:T(8,128)(2,1)} %param.19) | copy-start | bytes 98308
  46.4 1.5 %copy-start.13 = (f32[128]{0:T(128)S(1)}, f32[128]{0:T(128)}, u32[]{:S(2)}) copy-start(f32[128]{0:T(128)} %param.20) | copy-start | bytes 1540
  47.9 2.5 %copy-start.3 = (bf16[12,192,4,32]{1,3,0,2:T(8,128)(2,1)S(1)}, bf16[12,192,4,32]{1,3,0,2:T(8,128)(2,1)}, u32[]{:S(2)}) copy-start(bf16[12,192,4,32]{1,3,0,2:T(8,128)(2,1)} %copy.40) | copy-start | bytes 1769476
  55.3 2.9 %copy-start.2 = (f32[12,192,128]{2,1,0:T(8,128)S(1)}, f32[12,192,128]{2,1,0:T(8,128)}, u32[]{:S(2)}) copy-start(f32[12,192,128]{2,1,0:T(8,128)} %get-tuple-element.269) | copy-start | bytes 3538948 | tf_op jit(solution)/shard_map/while
  58.6 1.2 %copy-start.4 = (bf16[12,192,4,32]{1,3,0,2:T(8,128)(2,1)S(1)}, bf16[12,192,4,32]{1,3,0,2:T(8,128)(2,1)}, u32[]{:S(2)}) copy-start(bf16[12,192,4,32]{1,3,0,2:T(8,128)(2,1)} %get-tuple-element.292) | copy-start | bytes 1769476 | tf_op jit(solution)/shard_map/while
  64.7 2.9 %copy-start.2 = (f32[12,192,128]{2,1,0:T(8,128)S(1)}, f32[12,192,128]{2,1,0:T(8,128)}, u32[]{:S(2)}) copy-start(f32[12,192,128]{2,1,0:T(8,128)} %get-tuple-element.269) | copy-start | bytes 3538948 | tf_op jit(solution)/shard_map/while
  68.1 1.1 %copy-start.4 = (bf16[12,192,4,32]{1,3,0,2:T(8,128)(2,1)S(1)}, bf16[12,192,4,32]{1,3,0,2:T(8,128)(2,1)}, u32[]{:S(2)}) copy-start(bf16[12,192,4,32]{1,3,0,2:T(8,128)(2,1)} %get-tuple-element.292) | copy-start | bytes 1769476 | tf_op jit(solution)/shard_map/while
  69.2 15.4 %copy-start.5 = (bf16[128,128]{1,0:T(8,128)(2,1)S(1)}, bf16[128,128]{1,0:T(8,128)(2,1)}, u32[]{:S(2)}) copy-start(bf16[128,128]{1,0:T(8,128)(2,1)} %param.22) | copy-start | bytes 98308
  69.2 15.4 %copy-start.10 = (f32[128]{0:T(128)S(1)}, f32[128]{0:T(128)}, u32[]{:S(2)}) copy-start(f32[128]{0:T(128)} %param.23) | copy-start | bytes 1540
where the time goes:
time: 86.4 us; the launch traced here: 85.9 us
  blocking collectives  45.7 us (53%)
  matrix products  21 us (24%)
  local copies, waits for them, and re-layouts  9.81 us (11%)
  other arithmetic  4.24 us (5%)
  starting transfers between devices  4.24 us (5%)
    all_gather x1, blocking collectives, whole_row_layer(): bias_part = lax.all_gather(local_bias, 'cols', axis=1, tiled=True)  15.8 us
    all_to_all x1, blocking collectives, whole_row_layer(): lax.all_to_all(gated_all, 'rows', split_axis=1, concat_axis=0, tiled=True)  15.2 us
    all_gather x1, blocking collectives, whole_row_layer(): lax.all_gather(bias_part, 'rows', axis=2, tiled=True)  9.04 us
    sub x2, matrix products, one_block(): expo = jnp.exp(scores - highest)  8.86 us
    dot_general x2, matrix products, one_block(): jnp.einsum('hijk,ikhd->ijhd', weights, values, preferred_element_type=jnp...  5.81 us
    unnamed x1, blocking collectives  5.63 us
    all_to_all x1, starting transfers between devices, whole_row_layer(): lax.all_to_all(normed, 'rows', split_axis=0, concat_axis=1, tiled=True)  4.24 us
    dot_general x1, matrix products, whole_row_layer(): jnp.dot(normed.astype(jnp.float32), w_bias, precision=lax.Precision.HIGHEST)  2.85 us
  transfers between devices with their start and end apart: 1, of which 0 were waited for; matrix products, arithmetic and copies ran while one was open for 4% of the time, Pallas kernels for 0%

commit v1 on v0

--- a/solution.py
+++ b/solution.py
@@ -30,8 +30,18 @@
     wide = lax.all_to_all(normed, "rows", split_axis=0, concat_axis=1, tiled=True)
     few_rows, token_count, _ = wide.shape
     bias_part = lax.all_gather(local_bias, "cols", axis=1, tiled=True)
+
+    def _store_squares(w_in):
+        back = jnp.concatenate(
+            lax.all_to_all(
+                jnp.stack([w_in] * lax.axis_size("rows")), "rows", split_axis=0, concat_axis=0
+            ),
+            2,
+        )
+        return back
+
     full_bias, full_mask = (
-        lax.all_gather(bias_part, "rows", axis=2, tiled=True),
+        _store_squares(bias_part),
         lax.all_gather(token_mask.astype(jnp.float32), "rows", axis=0, tiled=True),
     )
     queries = (

time: 86.4 us -> 87.3 us (1.010)
  blocking collectives: 45.7 us -> 36.7 us
  starting transfers between devices: 4.24 us -> 7.74 us
  waiting for transfers between devices: 0.01 us -> 3.47 us
  local copies, waits for them, and re-layouts: 9.81 us -> 12.5 us
    all_gather x1 -> x0, blocking collectives: 9.04 us -> none  [whole_row_layer(): lax.all_gather(bias_part, 'rows', axis=2, tiled=True)]
    all_to_all x0 -> x1, starting transfers between devices: none -> 3.49 us  [_store_squares(): lax.all_to_all(jnp.stack([w_in] * lax.axis_size('rows')), 'rows', split_a...]
    all_to_all x0 -> x1, waiting for transfers between devices: none -> 3.47 us  [_store_squares(): lax.all_to_all(jnp.stack([w_in] * lax.axis_size('rows')), 'rows', split_a...]
    slice x1, local copies, waits for them, and re-layouts: 0.28 us -> 1.33 us  [whole_row_layer(): keys = keyvals[..., :width].reshape(few_rows, token_count, HEADS, HEAD_DIM)]
    another operation x0 -> x1, local copies, waits for them, and re-layouts: none -> 0.96 us  [_store_squares(): jnp.stack([w_in] * lax.axis_size('rows'))]
  transfers between devices with their start and end apart: 1 -> 2, of which waited for: 0 -> 1; matrix products, arithmetic and copies ran while one was open for 4% -> 14% of each run, Pallas kernels for 0% -> 0%
where the time goes in v1:
time: 87.3 us; the launch traced here: 86.7 us
  blocking collectives  36.7 us (42%)
  matrix products  21.1 us (24%)
  local copies, waits for them, and re-layouts  12.5 us (14%)
  starting transfers between devices  7.74 us (9%)
  other arithmetic  4.24 us (5%)
  waiting for transfers between devices  3.47 us (4%)
    all_gather x1, blocking collectives, whole_row_layer(): bias_part = lax.all_gather(local_bias, 'cols', axis=1, tiled=True)  15.8 us
    all_to_all x1, blocking collectives, whole_row_layer(): lax.all_to_all(gated_all, 'rows', split_axis=1, concat_axis=0, tiled=True)  15.2 us
    sub x2, matrix products, one_block(): expo = jnp.exp(scores - highest)  8.96 us
    dot_general x2, matrix products, one_block(): jnp.einsum('hijk,ikhd->ijhd', weights, values, preferred_element_type=jnp...  5.81 us
    unnamed x1, blocking collectives  5.63 us
    all_to_all x1, starting transfers between devices, whole_row_layer(): lax.all_to_all(normed, 'rows', split_axis=0, concat_axis=1, tiled=True)  4.24 us
    all_to_all x1, starting transfers between devices, _store_squares(): lax.all_to_all(jnp.stack([w_in] * lax.axis_size('rows')), 'rows', split_a...  3.49 us
    all_to_all x1, waiting for transfers between devices, _store_squares(): lax.all_to_all(jnp.stack([w_in] * lax.axis_size('rows')), 'rows', split_a...  3.47 us
  transfers between devices with their start and end apart: 2, of which 1 were waited for; matrix products, arithmetic and copies ran while one was open for 14% of the time, Pallas kernels for 0%

profile of v1, /device:TPU:0, one launch (start us, length us, event | category | flops | bytes accessed | tf_op | source)
XLA Modules:
  0.0 86.7 jit_solution(13453615707136362202)
XLA Ops:
  0.0 0.0 copy-start
  0.0 1.7 %reduce_sum.31 = f32[48,48]{1,0:T(8,128)S(1)} reduce(f32[48,48,128]{2,1,0:T(8,128)} %param.13, f32[]{:T(128)} %constant.58.clone.1), dimensions={2}, to_apply=%region_0.0 | reduce | flops 292608 | bytes 1188868 | tf_op jit(solution)/shard_map/reduce_sum | solution.py:11
  1.8 0.0 copy-done.1
  1.8 0.7 multiply_reduce_fusion
  2.5 0.0 copy-done.9
  2.5 0.0 copy-done.8
  2.5 0.0 copy-start.7
  2.5 1.5 %add_convert_fusion = bf16[48,48,128]{2,1,0:T(8,128)(2,1)} fusion(f32[48,48,128]{2,1,0:T(8,128)S(1)} %copy-done.1, f32[128]{0:T(128)S(1)} %copy-done.8, f32[128]{0:T(128)S(1)} %copy-done.9, f32[48,48]{1,0:T(8,128)S(1)} %add_rsqrt_fusion, f32[48,48]{1,0:T(8,128)S(1)} %broadcast_multiply_fusion), kind=kLoop, calls=%fused_computation.31 | loop fusion | flops 1474560 | bytes 1788928 | tf_op jit(solution)/shard_map/convert_element_type | solution.py:14
  4.0 4.2 %all-to-all-start = ((bf16[48,48,128]{2,1,0:T(8,128)(2,1)}), bf16[48,48,128]{2,1,0:T(8,128)(2,1)S(1)}, u32[]{:S(2)}, u32[]{:S(2)}) async-start(bf16[48,48,128]{2,1,0:T(8,128)(2,1)} %add_convert_fusion), calls=%async_computation | async-start | bytes 1179648 | tf_op jit(solution)/shard_map/all_to_all | solution.py:30
  8.3 0.0 copy-done.7
  8.3 2.8 %convolution_bitcast_fusion = f32[4,48,48]{2,0,1:T(4,128)S(1)} fusion(bf16[48,48,128]{2,1,0:T(8,128)(2,1)} %add_convert_fusion, f32[128,4]{0,1:T(4,128)S(1)} %copy-done.7), kind=kOutput, calls=%fused_computation.33 | convolution fusion | flops 14155776 | bytes 628736 | tf_op jit(solution)/shard_map/dot_general | solution.py:27
  11.1 15.8 %all_gather.7 = f32[4,192,48]{2,0,1:T(4,128)S(1)} all-gather(f32[4,48,48]{2,0,1:T(4,128)S(1)} %convolution_bitcast_fusion), channel_id=1, replica_groups=mesh['groups'=2,'rows'=4,'cols'=4] {'cols'}, dimensions={1}, use_global_device_ids=true | all-gather | bytes 184320 | tf_op jit(solution)/shard_map/all_gather | solution.py:32
  27.0 0.2 copy.37
  27.1 0.0 copy-done.14
  27.2 0.6 dynamic-slice
  28.3 0.0 copy-done.12
  28.3 0.1 convert_dynamic-update-slice_fusion
  28.4 5.6 %all-reduce = f32[192]{0:T(256)S(1)} all-reduce(f32[192]{0:T(256)S(1)} %convert_dynamic-update-slice_fusion), channel_id=1, replica_groups=mesh['groups'=2,'rows'=4,'cols'=4] {'rows'}, use_global_device_ids=true, to_apply=%add | all-reduce | flops 192 | bytes 1536
  34.1 0.0 all-to-all-done
  34.1 1.0 %stack.2 = f32[4,4,192,48]{2,3,1,0:T(8,128)} broadcast(f32[4,192,48]{1,2,0:T(8,128)S(1)} %copy.37), dimensions={1,2,3} | broadcast | bytes 737280 | tf_op jit(solution)/shard_map/stack | solution.py:37
  35.0 3.5 %all-to-all-start.1 = ((f32[4,4,192,48]{2,3,1,0:T(8,128)}), f32[4,4,192,48]{2,3,1,0:T(8,128)S(1)}, u32[]{:S(2)}, u32[]{:S(2)}) async-start(f32[4,4,192,48]{2,3,1,0:T(8,128)} %stack.2), calls=%async_computation.1 | async-start | bytes 1572864 | tf_op jit(solution)/shard_map/all_to_all | solution.py:36
  38.5 0.1 copy.34
  38.6 0.0 copy-done
  38.6 0.4 convolution_convert_fusion
  39.0 1.1 %fusion.39 = (bf16[12,192,128]{2,1,0:T(8,128)(2,1)S(1)}, bf16[12,192,128]{2,1,0:T(8,128)(2,1)}) fusion(bf16[12,192,256]{2,1,0:T(8,128)(2,1)S(1)} %convolution_convert_fusion), kind=kLoop, calls=%fused_computation.44 | loop fusion | bytes 2359296 | tf_op jit(solution)/shard_map/slice | solution.py:53
  40.2 1.3 %copy.36 = bf16[12,192,128]{1,2,0:T(8,128)(2,1)S(1)} copy(bf16[12,192,128]{2,1,0:T(8,128)(2,1)} %get-tuple-element.189) | data formatting | bytes 1179648 | tf_op jit(solution)/shard_map/slice | solution.py:52
  41.5 0.0 copy-start.6
  41.5 0.9 %copy.42 = bf16[12,192,4,32]{1,3,0,2:T(8,128)(2,1)} copy(bf16[12,192,4,32]{1,3,2,0:T(8,128)(2,1)S(1)} %bitcast.63) | data formatting | bytes 1179648 | tf_op jit(solution)/shard_map/while | solution.py:77
  42.5 1.2 %copy.39 = bf16[12,192,128]{1,2,0:T(8,128)(2,1)} copy(bf16[12,192,128]{2,1,0:T(8,128)(2,1)S(1)} %get-tuple-element.188) | data formatting | bytes 1179648 | tf_op jit(solution)/shard_map/slice | solution.py:53
  43.7 0.0 copy-done.6
  43.7 0.3 fusion.28
  44.0 1.2 %copy.35 = bf16[12,192,128]{1,2,0:T(8,128)(2,1)} copy(bf16[12,192,128]{2,1,0:T(8,128)(2,1)S(1)} %fusion.28) | data formatting | bytes 1179648 | tf_op jit(solution)/shard_map/convert_element_type | solution.py:49
  45.2 0.0 copy-done.11
  45.2 0.0 copy-done.13
  45.2 1.5 %fusion.27 = f32[12,192,128]{2,1,0:T(8,128)} fusion(bf16[12,192,128]{2,1,0:T(8,128)(2,1)S(1)} %bitcast.62, f32[128]{0:T(128)S(1)} %copy-done.13, bf16[128,128]{1,0:T(8,128)(2,1)S(1)} %copy-done.11), kind=kOutput, calls=%fused_computation.29 | convolution fusion | flops 76677120 | bytes 1802752 | tf_op jit(solution)/shard_map/dot_general | solution.py:54
  46.6 3.5 %all-to-all-done.1 = f32[4,4,192,48]{2,3,1,0:T(8,128)S(1)} async-done(((f32[4,4,192,48]{2,3,1,0:T(8,128)}), f32[4,4,192,48]{2,3,1,0:T(8,128)S(1)}, u32[]{:S(2)}, u32[]{:S(2)}) %all-to-all-start.1) | async-done | bytes 589856 | tf_op jit(solution)/shard_map/all_to_all | solution.py:36
  50.1 0.1 copy.38
  50.2 1.0 %broadcast_in_dim.45.clone = bf16[12,192,128]{2,0,1:T(8,128)(2,1)} broadcast(bf16[]{:T(256)} %constant.57.clone.1), dimensions={} | broadcast | bytes 589826 | tf_op jit(solution)/shard_map/broadcast_in_dim | solution.py:81
  51.2 0.0 copy-done.3
  51.2 18.8 %while.13 = (s32[]{:T(128)}, bf16[12,192,128]{2,0,1:T(8,128)(2,1)}, f32[12,192,128]{2,1,0:T(8,128)}, pred[192]{0:T(512)(128)(4,1)S(1)}, bf16[12,192,4,32]{1,3,2,...) while((s32[]{:T(128)}, bf16[12,192,128]{2,0,1:T(8,128)(2,1)}, ...), condition=%wide.region_5.6_spmd, body=%wide.region_2.5_spmd.sunk | while | flops 118112448 | bytes 19440052 | solution.py:77
  51.2 0.2 constant_dynamic-slice_fusion.13
  51.4 0.2 copy.80
  51.6 4.5 %fusion.59 = (f32[4,12,96]{2,1,0:T(8,128)S(1)}, bf16[4,12,96,192]{3,2,1,0:T(8,128)(2,1)}) fusion(f32[4,96,192]{2,1,0:T(8,128)S(1)} %copy.80, pred[192]{0:T(512)(128)(4,1)S(1)} %get-tuple-element.270, bf16[12,192,4,32]{1,3,0,2:T(8,128)(2,1)S(1)} %get-tuple-element.272, bf16[12,192,4,32]{1,3,2,0:T(8,128)(2,1)} %get-tuple-element.271, s32[]{:T(128)S(6)} %select_n.31), kind=kOutput, calls=%fused_computation.43.clone.1 | convolution fusion | flops 61046976 | bytes 3066052 | tf_op jit(solution)/shard_map/while/body/eval_jaxpr/sub | solution.py:69
  56.1 0.0 copy-start.2
  56.1 2.9 %fusion.60 = f32[12,96,4,32]{1,3,2,0:T(8,128)S(1)} fusion(bf16[12,192,4,32]{1,3,2,0:T(8,128)(2,1)} %get-tuple-element.274, bf16[4,12,96,192]{3,2,1,0:T(8,128)(2,1)} %get-tuple-element.241, f32[12,96,4]{1,2,0:T(4,128)S(1)} %copy.81), kind=kOutput, calls=%fused_computation.10.clone.1 | convolution fusion | flops 56770560 | bytes 2967552 | tf_op jit(solution)/shard_map/while/body/eval_jaxpr/hijk,ikhd->ijhd/dot_general | solution.py:72
  59.0 0.0 copy-done.2
  59.0 0.1 constant_dynamic-slice_fusion.12
  59.0 0.3 copy.79
  59.3 0.1 fusion.61
  59.4 0.4 copy.82
  59.8 0.8 constant_dynamic-update-slice_fusion.2
  60.6 0.2 constant_dynamic-slice_fusion.13
  60.8 0.2 copy.80
  61.0 4.5 %fusion.59 = (f32[4,12,96]{2,1,0:T(8,128)S(1)}, bf16[4,12,96,192]{3,2,1,0:T(8,128)(2,1)}) fusion(f32[4,96,192]{2,1,0:T(8,128)S(1)} %copy.80, pred[192]{0:T(512)(128)(4,1)S(1)} %get-tuple-element.270, bf16[12,192,4,32]{1,3,0,2:T(8,128)(2,1)S(1)} %get-tuple-element.272, bf16[12,192,4,32]{1,3,2,0:T(8,128)(2,1)} %get-tuple-element.271, s32[]{:T(128)S(6)} %select_n.31), kind=kOutput, calls=%fused_computation.43.clone.1 | convolution fusion | flops 61046976 | bytes 3066052 | tf_op jit(solution)/shard_map/while/body/eval_jaxpr/sub | solution.py:69
  65.5 0.0 copy-start.2
  65.5 2.9 %fusion.60 = f32[12,96,4,32]{1,3,2,0:T(8,128)S(1)} fusion(bf16[12,192,4,32]{1,3,2,0:T(8,128)(2,1)} %get-tuple-element.274, bf16[4,12,96,192]{3,2,1,0:T(8,128)(2,1)} %get-tuple-element.241, f32[12,96,4]{1,2,0:T(4,128)S(1)} %copy.81), kind=kOutput, calls=%fused_computation.10.clone.1 | convolution fusion | flops 56770560 | bytes 2967552 | tf_op jit(solution)/shard_map/while/body/eval_jaxpr/hijk,ikhd->ijhd/dot_general | solution.py:72
  68.4 0.1 constant_dynamic-slice_fusion.12
  68.4 0.3 copy.79
  68.7 0.1 fusion.61
  68.8 0.4 copy.82
  69.2 0.8 constant_dynamic-update-slice_fusion.2
  70.0 15.2 %all_to_all.41 = bf16[12,192,128]{2,0,1:T(8,128)(2,1)S(1)} all-to-all(bf16[12,192,128]{2,0,1:T(8,128)(2,1)} %get-tuple-element.282), channel_id=1, replica_groups=mesh['groups'=2,'rows'=4,'cols'=4] {'rows'}, dimensions={1} | all-to-all | bytes 1179648 | tf_op jit(solution)/shard_map/all_to_all | solution.py:83
  85.2 0.2 copy.46
  85.4 1.3 %convolution_add_fusion = f32[48,48,128]{2,1,0:T(8,128)} fusion(bf16[48,48,128]{2,1,0:T(8,128)(2,1)S(1)} %bitcast.66, f32[128]{0:T(128)S(1)} %copy-done.10, bf16[128,128]{1,0:T(8,128)(2,1)S(1)} %copy-done.5), kind=kOutput, calls=%fused_computation.23 | convolution fusion | flops 75792384 | bytes 1802752 | tf_op jit(solution)/shard_map/dot_general | solution.py:84
  (23 shorter events, 0.1 us)
Async XLA Ops:
  0.0 38.6 %copy-start = (bf16[128,256]{1,0:T(8,128)(2,1)S(1)}, bf16[128,256]{1,0:T(8,128)(2,1)}, u32[]{:S(2)}) copy-start(bf16[128,256]{1,0:T(8,128)(2,1)} %param.18) | copy-start | bytes 196612
  0.0 1.8 %copy-start.1 = (f32[48,48,128]{2,1,0:T(8,128)S(1)}, f32[48,48,128]{2,1,0:T(8,128)}, u32[]{:S(2)}) copy-start(f32[48,48,128]{2,1,0:T(8,128)} %param.13) | copy-start | bytes 3538948
  0.0 2.5 %copy-start.9 = (f32[128]{0:T(128)S(1)}, f32[128]{0:T(128)}, u32[]{:S(2)}) copy-start(f32[128]{0:T(128)} %param.15) | copy-start | bytes 1540
  0.0 2.5 %copy-start.8 = (f32[128]{0:T(128)S(1)}, f32[128]{0:T(128)}, u32[]{:S(2)}) copy-start(f32[128]{0:T(128)} %param.16) | copy-start | bytes 1540
  2.5 5.8 %copy-start.7 = (f32[128,4]{0,1:T(4,128)S(1)}, f32[128,4]{0,1:T(4,128)}, u32[]{:S(2)}) copy-start(f32[128,4]{0,1:T(4,128)} %param.21) | copy-start | bytes 6148
  4.0 30.0 %all-to-all-start = ((bf16[48,48,128]{2,1,0:T(8,128)(2,1)}), bf16[48,48,128]{2,1,0:T(8,128)(2,1)S(1)}, u32[]{:S(2)}, u32[]{:S(2)}) async-start(bf16[48,48,128]{2,1,0:T(8,128)(2,1)} %add_convert_fusion), calls=%async_computation | async-start | bytes 1179648 | tf_op jit(solution)/shard_map/all_to_all | solution.py:30
  8.3 18.9 %copy-start.14 = (u32[32]{0:T(128)S(1)}, u32[32]{0:T(128)}, u32[]{:S(2)}) copy-start(u32[32]{0:T(128)} %constant.66) | copy-start | bytes 388
  8.3 20.0 %copy-start.12 = (s32[48]{0:T(128)S(1)}, s32[48]{0:T(128)}, u32[]{:S(2)}) copy-start(s32[48]{0:T(128)} %param.14) | copy-start | bytes 580
  35.0 15.1 %all-to-all-start.1 = ((f32[4,4,192,48]{2,3,1,0:T(8,128)}), f32[4,4,192,48]{2,3,1,0:T(8,128)S(1)}, u32[]{:S(2)}, u32[]{:S(2)}) async-start(f32[4,4,192,48]{2,3,1,0:T(8,128)} %stack.2), calls=%async_computation.1 | async-start | bytes 1572864 | tf_op jit(solution)/shard_map/all_to_all | solution.py:36
  41.5 2.1 %copy-start.6 = (bf16[128,128]{1,0:T(8,128)(2,1)S(1)}, bf16[128,128]{1,0:T(8,128)(2,1)}, u32[]{:S(2)}) copy-start(bf16[128,128]{1,0:T(8,128)(2,1)} %param.17) | copy-start | bytes 98308
  43.7 1.5 %copy-start.11 = (bf16[128,128]{1,0:T(8,128)(2,1)S(1)}, bf16[128,128]{1,0:T(8,128)(2,1)}, u32[]{:S(2)}) copy-start(bf16[128,128]{1,0:T(8,128)(2,1)} %param.19) | copy-start | bytes 98308
  43.7 1.5 %copy-start.13 = (f32[128]{0:T(128)S(1)}, f32[128]{0:T(128)}, u32[]{:S(2)}) copy-start(f32[128]{0:T(128)} %param.20) | copy-start | bytes 1540
  46.6 4.5 %copy-start.3 = (bf16[12,192,4,32]{1,3,0,2:T(8,128)(2,1)S(1)}, bf16[12,192,4,32]{1,3,0,2:T(8,128)(2,1)}, u32[]{:S(2)}) copy-start(bf16[12,192,4,32]{1,3,0,2:T(8,128)(2,1)} %copy.42) | copy-start | bytes 1769476
  56.1 2.9 %copy-start.2 = (f32[12,192,128]{2,1,0:T(8,128)S(1)}, f32[12,192,128]{2,1,0:T(8,128)}, u32[]{:S(2)}) copy-start(f32[12,192,128]{2,1,0:T(8,128)} %get-tuple-element.269) | copy-start | bytes 3538948 | tf_op jit(solution)/shard_map/while
  59.4 1.2 %copy-start.4 = (bf16[12,192,4,32]{1,3,0,2:T(8,128)(2,1)S(1)}, bf16[12,192,4,32]{1,3,0,2:T(8,128)(2,1)}, u32[]{:S(2)}) copy-start(bf16[12,192,4,32]{1,3,0,2:T(8,128)(2,1)} %get-tuple-element.293) | copy-start | bytes 1769476 | tf_op jit(solution)/shard_map/while
  65.5 2.9 %copy-start.2 = (f32[12,192,128]{2,1,0:T(8,128)S(1)}, f32[12,192,128]{2,1,0:T(8,128)}, u32[]{:S(2)}) copy-start(f32[12,192,128]{2,1,0:T(8,128)} %get-tuple-element.269) | copy-start | bytes 3538948 | tf_op jit(solution)/shard_map/while
  68.8 1.2 %copy-start.4 = (bf16[12,192,4,32]{1,3,0,2:T(8,128)(2,1)S(1)}, bf16[12,192,4,32]{1,3,0,2:T(8,128)(2,1)}, u32[]{:S(2)}) copy-start(bf16[12,192,4,32]{1,3,0,2:T(8,128)(2,1)} %get-tuple-element.293) | copy-start | bytes 1769476 | tf_op jit(solution)/shard_map/while
  70.0 15.4 %copy-start.5 = (bf16[128,128]{1,0:T(8,128)(2,1)S(1)}, bf16[128,128]{1,0:T(8,128)(2,1)}, u32[]{:S(2)}) copy-start(bf16[128,128]{1,0:T(8,128)(2,1)} %param.22) | copy-start | bytes 98308
  70.0 15.4 %copy-start.10 = (f32[128]{0:T(128)S(1)}, f32[128]{0:T(128)}, u32[]{:S(2)}) copy-start(f32[128]{0:T(128)} %param.23) | copy-start | bytes 1540
